TPU v7x, 512 devices: a whole 4x4x16 slice. The times are simulated.
512 devices in a mesh: segment: 4 (over x_hi, core), seq: 32 (over x_lo, z), dp: 4 (over y).
Axes of the slice: x: 4 (x_hi: 2, x_lo: 2; x = x_hi * 2 + x_lo), y: 4, z: 16, core: 2. Of those that a mesh axis runs over, the one named last changes fastest.
Arguments:
- q_in: bfloat16 [4, 4096, 1536], P('dp', 'seq', 'segment'), may hold values from -128 to 128
- k_in: bfloat16 [4, 4096, 1536], P('dp', 'seq', 'segment'), may hold values from -128 to 128
- v_in: bfloat16 [4, 4096, 1536], P('dp', 'seq', 'segment'), may hold values from -6 to 6
- q_gain: float32 [2, 64], replicated, may hold values from 1.5 to 4
- gate: float32 [768], replicated, may hold values from -6 to 6
- cot: bfloat16 [4, 4096, 768], P('dp', 'seq'), may hold values from -6 to 6
Outputs:
- attn_out: bfloat16 [4, 4096, 1536], P('dp', 'seq', 'segment')
- grad_gate: float32 [768], replicated
All inputs are finite; a program needn't handle non-finite values.
Results may differ from a plain program's by a relative error of at most 0.028.
The roundings to bfloat16 on the way count: a program that leaves them out, or rounds other values in their place, can miss the bound.
Values may be sent and summed in bfloat16 or wider, within the bound.
A program may use at most 64 MiB of HBM per device.

v0:
```python
import jax
import jax.numpy as jnp
from jax import lax
from jax.sharding import PartitionSpec as P

HEAD_DIM = 64


def shifted(value, axis, steps):
    count = lax.axis_size(axis)
    first, last = (max(0, -steps), min(count, count - steps))
    return lax.ppermute(value, axis, [(source, source + steps) for source in range(first, last)])


def attend(query, all_keys, all_values):
    count_rows = query.shape[0]
    total_keys = all_keys.shape[0]
    span = 2 * HEAD_DIM
    pieces = []
    probs_list = []
    totals_list = []
    for offset in range(0, query.shape[1], span):
        query_group = query[:, offset : offset + span].reshape(count_rows, 2, HEAD_DIM)
        keys_group = all_keys[:, offset : offset + span].reshape(total_keys, 2, HEAD_DIM)
        values_group = all_values[:, offset : offset + span].reshape(total_keys, 2, HEAD_DIM)
        scores = jnp.einsum(
            "qhd,khd->hqk", query_group, keys_group, preferred_element_type=jnp.float32
        ) * HEAD_DIM ** (-0.5)
        peak = jnp.max(scores, axis=-1, keepdims=True)
        expd = jnp.exp(scores - peak)
        total = jnp.sum(expd, axis=-1, keepdims=True)
        probs = expd.astype(jnp.bfloat16)
        result = jnp.einsum("hqk,khd->qhd", probs, values_group, preferred_element_type=jnp.float32)
        result = result / jnp.transpose(total, (1, 0, 2))
        pieces.append(result.reshape(count_rows, span))
        probs_list.append(probs)
        totals_list.append(total)
    return (jnp.concatenate(pieces, axis=1), probs_list, totals_list)


def attend_back(probs_list, totals_list, normed, upstream, all_keys, all_values):
    count_rows = upstream.shape[0]
    total_keys = all_keys.shape[0]
    span = 2 * HEAD_DIM
    pieces = []
    for number in range(len(probs_list)):
        offset = number * span
        upstream_group = upstream[:, offset : offset + span].reshape(count_rows, 2, HEAD_DIM)
        normed_group = normed[:, offset : offset + span].reshape(count_rows, 2, HEAD_DIM)
        keys_group = all_keys[:, offset : offset + span].reshape(total_keys, 2, HEAD_DIM)
        values_group = all_values[:, offset : offset + span].reshape(total_keys, 2, HEAD_DIM)
        dprob = jnp.einsum(
            "qhd,khd->hqk", upstream_group, values_group, preferred_element_type=jnp.float32
        )
        delta = jnp.sum(upstream_group.astype(jnp.float32) * normed_group, axis=-1)
        delta = jnp.transpose(delta, (1, 0))[:, :, None]
        dscore = (
            probs_list[number].astype(jnp.float32) / totals_list[number] * (dprob - delta)
        ).astype(jnp.bfloat16)
        result = jnp.einsum(
            "hqk,khd->qhd", dscore, keys_group, preferred_element_type=jnp.float32
        ) * HEAD_DIM ** (-0.5)
        pieces.append(result.reshape(count_rows, span))
    return jnp.concatenate(pieces, axis=1)


def local(q_in, k_in, v_in, q_gain, gate, cot):
    half = lax.axis_size("segment") // 2
    place = lax.axis_index("segment")
    is_main = place >= half
    section = place // half
    slot = place % half
    queries = q_in[0]
    keys = k_in[0]
    values = v_in[0]
    count_rows = queries.shape[0]
    width_dev = queries.shape[1]
    all_keys, all_values = (
        lax.all_gather(keys, "seq", axis=0, tiled=True),
        lax.all_gather(values, "seq", axis=0, tiled=True),
    )
    gain_row = lax.dynamic_slice_in_dim(q_gain, section, 1, 0)[0]
    gate_part = lax.dynamic_slice_in_dim(gate, slot * width_dev, width_dev, 0)
    cot_part = lax.dynamic_slice_in_dim(cot[0], slot * width_dev, width_dev, 1)
    raw = queries.astype(jnp.float32).reshape(count_rows, width_dev // HEAD_DIM, HEAD_DIM)
    unit = raw * lax.rsqrt(jnp.mean(raw * raw, axis=-1, keepdims=True) + 1e-06)
    base = (unit * gain_row).reshape(count_rows, width_dev)

    def control_run(base_in):
        normed_c = attend(base_in.astype(jnp.bfloat16), all_keys, all_values)[0]
        return lax.optimization_barrier(normed_c.astype(jnp.bfloat16))

    def control_skip(base_in):
        return jnp.zeros((count_rows, width_dev), jnp.bfloat16)

    first = lax.cond(is_main, control_skip, control_run, base)
    first_wide = first.astype(jnp.float32)
    outgoing = (gate_part * first_wide).astype(jnp.bfloat16)
    incoming = shifted(outgoing, "segment", half)

    def main_run(incoming_in):
        query = (base + incoming_in.astype(jnp.float32)).astype(jnp.bfloat16)
        normed_m, probs_list, totals_list = attend(query, all_keys, all_values)
        dquery = attend_back(probs_list, totals_list, normed_m, cot_part, all_keys, all_values)
        return (normed_m.astype(jnp.bfloat16), dquery)

    def main_skip(incoming_in):
        return (
            jnp.zeros((count_rows, width_dev), jnp.bfloat16),
            jnp.zeros((count_rows, width_dev), jnp.float32),
        )

    final, dquery_main = lax.cond(is_main, main_run, main_skip, incoming)
    returned = shifted(dquery_main.astype(jnp.bfloat16), "segment", -half)
    returned_wide = returned.astype(jnp.float32)
    part_gate = jnp.sum(first_wide * returned_wide, axis=0)
    placed = lax.dynamic_update_slice_in_dim(
        jnp.zeros((width_dev * half,), jnp.float32), part_gate, slot * width_dev, 0
    )
    total_gate = lax.psum(placed, ("segment", "seq", "dp"))
    output = jnp.where(is_main, final, first)
    return (output[None], total_gate)


def solution(mesh):
    in_specs = (
        P("dp", "seq", "segment"),
        P("dp", "seq", "segment"),
        P("dp", "seq", "segment"),
        P(),
        P(),
        P("dp", "seq", None),
    )
    out_specs = (P("dp", "seq", "segment"), P())
    return jax.shard_map(local, mesh=mesh, in_specs=in_specs, out_specs=out_specs, check_vma=False)
```

profile of v0, /device:TPU:1, one launch (start us, length us, event | category | flops | bytes accessed | tf_op | source)
XLA Modules:
  0.0 449.7 jit_solution(1224437534765963869)
XLA Ops:
  7.2 0.0 copy-start
  7.2 0.0 all-gather.5.cloned.1.call-start
  7.2 1.6 copy.10
  8.9 0.0 all-gather.5.cloned.1.call-update
  8.9 0.0 all-gather.7.cloned.1.call-start
  8.9 1.6 copy.11
  10.6 0.0 all-gather.7.cloned.1.call-update
  10.6 0.0 copy-done
  10.6 0.1 mul.127
  10.7 1.0 copy.9
  11.8 0.1 fusion.70
  11.9 0.8 dynamic_slice.11
  12.7 116.3 %all-gather.5.cloned.1.call-done = bf16[1,4096,384]{1,2,0:T(8,128)(2,1)} async-done(((bf16[1,128,384]{1,2,0:T(8,128)(2,1)}), bf16[1,4096,384]{1,2,0:T(8,128)(2,1)}) %all-gather.5.cloned.1.call-update) | async-done | bytes 3145744 | tf_op jit(solution)/shard_map/all_gather | solution.py:79
  129.0 133.1 %all-gather.7.cloned.1.call-done = bf16[1,4096,384]{1,2,0:T(8,128)(2,1)} async-done(((bf16[1,128,384]{1,2,0:T(8,128)(2,1)}), bf16[1,4096,384]{1,2,0:T(8,128)(2,1)}) %all-gather.7.cloned.1.call-update) | async-done | bytes 3145744 | tf_op jit(solution)/shard_map/all_gather | solution.py:80
  262.1 10.9 %conditional.2 = (f32[128,384]{0,1:T(8,128)S(1)}, bf16[128,384]{1,0:T(8,128)(2,1)S(1)}) conditional(s32[]{:T(128)} %convert_element_type.105, (f32[128,384]{0,1:T(8,128)S(1)}, bf16[4096,384]{0,1:T(8,128)(2,1)}, bf16[4096,384]{0,1:T(8,128)(2,1)}) %tuple.81, () %tuple.30), branch_computations={%region_1.8_spmd, %region_8.9_spmd} | conditional | flops 824670720 | bytes 58014736 | solution.py:96
  262.1 3.2 fusion.71
  265.4 0.8 fusion.76
  266.2 0.7 fusion
  267.0 0.9 fusion.39
  267.9 0.8 fusion.75
  268.7 0.7 fusion.2
  269.4 0.9 fusion.36
  270.4 0.8 fusion.74
  271.2 0.7 fusion.4
  271.9 0.9 fusion.33
  272.9 0.1 copy.15
  273.1 0.0 copy-start.6
  273.1 0.1 multiply_convert_fusion
  273.2 1.3 collective-permute-start
  274.5 1.6 collective-permute-done
  276.1 0.0 copy-done.6
  276.1 0.9 conditional.3
  276.1 0.7 broadcast.53.clone
  277.0 1.3 collective-permute-start.1
  278.3 1.6 select_bitcast_fusion
  279.8 38.2 %collective-permute-done.1 = bf16[128,384]{0,1:T(8,128)(2,1)S(1)} collective-permute-done((bf16[128,384]{0,1:T(8,128)(2,1)S(1)}, bf16[128,384]{0,1:T(8,128)(2,1)S(1)}, u32[]{:S(2)}, u32[]{:S(2)}) %collective-permute-start.1) | collective-permute-done | bytes 98336 | tf_op jit(solution)/shard_map/ppermute | solution.py:12
  318.0 0.1 multiply_reduce_fusion.3
  318.2 0.2 dynamic_update_slice.3
  318.5 124.4 %psum.7 = f32[768]{0:T(1024)} all-reduce(f32[768]{0:T(1024)S(1)} %dynamic_update_slice.3), channel_id=1, replica_groups=mesh['segment'=4,'seq'=32,'dp'=4] {'segment','seq','dp'}, use_global_device_ids=true, to_apply=%region_21.22 | all-reduce | flops 768 | bytes 6144 | tf_op jit(solution)/shard_map/psum | solution.py:120
  (11 shorter events, 0.1 us)
Async XLA Ops:
  7.2 3.4 copy-start
  7.2 121.8 %all-gather.5.cloned.1.call-start = ((), (), s32[]{:S(2)}) async-start(), calls=%async_computation | async-start | bytes 3244032 | tf_op jit(solution)/shard_map/all_gather | solution.py:79
  8.9 253.3 %all-gather.7.cloned.1.call-start = ((), (), s32[]{:S(2)}) async-start(), calls=%async_computation.1 | async-start | bytes 3244032 | tf_op jit(solution)/shard_map/all_gather | solution.py:80
  273.1 3.1 copy-start.6
  273.2 2.9 collective-permute-start
  277.0 41.1 %collective-permute-start.1 = (bf16[128,384]{0,1:T(8,128)(2,1)S(1)}, bf16[128,384]{0,1:T(8,128)(2,1)S(1)}, u32[]{:S(2)}, u32[]{:S(2)}) collective-permute-start(bf16[128,384]{0,1:T(8,128)(2,1)S(1)} %get-tuple-element.53), channel_id=1, source_target_pairs={{256,0},{384,128},{257,1},{385,129},{258,2},{386,130},{259,3},{387... | collective-permute-start | bytes 294920 | tf_op jit(solution)/shard_map/ppermute | solution.py:12
Sparse Core Ops, SparseCore 0:
  10.6 118.3 all-gather.4
  131.0 131.0 all-gather.6
where the time goes:
time: 450 us
  waiting for transfers between devices  289 us (64%)
  blocking collectives  124 us (28%)
  between operations  14.2 us (3%)
  local copies, waits for them, and re-layouts  9.4 us (2%)
  matrix products  5.29 us (1%)
    all_gather x1, waiting for transfers between devices, local(): lax.all_gather(values, 'seq', axis=0, tiled=True)  133 us
    psum x1, blocking collectives, local(): total_gate = lax.psum(placed, ('segment', 'seq', 'dp'))  124 us
    all_gather x1, waiting for transfers between devices, local(): lax.all_gather(keys, 'seq', axis=0, tiled=True)  116 us
    ppermute x2, waiting for transfers between devices, shifted(): lax.ppermute(value, axis, [(source, source + steps) for source in range(f...  39.8 us
  transfers between devices with their start and end apart: 4, of which 4 were waited for; matrix products, arithmetic and copies ran while one was open for 1% of the time, Pallas kernels for 0%

commit v1 on v0

--- a/solution.py
+++ b/solution.py
@@ -117,7 +117,7 @@
     placed = lax.dynamic_update_slice_in_dim(
         jnp.zeros((width_dev * half,), jnp.float32), part_gate, slot * width_dev, 0
     )
-    total_gate = lax.psum(placed, ("segment", "seq", "dp"))
+    total_gate = lax.psum(lax.psum(placed, "segment"), ("seq", "dp"))
     output = jnp.where(is_main, final, first)
     return (output[None], total_gate)
 

time: 450 us -> 664 us (1.48)
  the two profiles are of different devices: /device:TPU:1 before, /device:TPU:2 now
where the time goes in v1:
time: 664 us
  blocking collectives  316 us (48%)
  waiting for transfers between devices  312 us (47%)
  between operations  14.2 us (2%)
  local copies, waits for them, and re-layouts  9.4 us (1%)
    psum x2, blocking collectives, local(): total_gate = lax.psum(lax.psum(placed, 'segment'), ('seq', 'dp'))  316 us
    all_gather x1, waiting for transfers between devices, local(): lax.all_gather(keys, 'seq', axis=0, tiled=True)  137 us
    all_gather x1, waiting for transfers between devices, local(): lax.all_gather(values, 'seq', axis=0, tiled=True)  133 us
    ppermute x2, waiting for transfers between devices, shifted(): lax.ppermute(value, axis, [(source, source + steps) for source in range(f...  41.6 us
  transfers between devices with their start and end apart: 4, of which 4 were waited for; matrix products, arithmetic and copies ran while one was open for 1% of the time, Pallas kernels for 0%

profile of v1, /device:TPU:2, one launch (start us, length us, event | category | flops | bytes accessed | tf_op | source)
XLA Modules:
  0.0 663.8 jit_solution(7789718472452773892)
XLA Ops:
  7.2 0.0 copy-start
  7.2 0.0 all-gather.5.cloned.1.call-start
  7.2 1.6 copy.10
  8.9 0.0 all-gather.5.cloned.1.call-update
  8.9 0.0 all-gather.7.cloned.1.call-start
  8.9 1.6 copy.11
  10.6 0.0 all-gather.7.cloned.1.call-update
  10.6 0.0 copy-done
  10.6 0.1 mul.127
  10.7 1.0 copy.9
  11.8 0.1 fusion.70
  11.9 0.8 dynamic_slice.11
  12.7 137.4 %all-gather.5.cloned.1.call-done = bf16[1,4096,384]{1,2,0:T(8,128)(2,1)} async-done(((bf16[1,128,384]{1,2,0:T(8,128)(2,1)}), bf16[1,4096,384]{1,2,0:T(8,128)(2,1)}) %all-gather.5.cloned.1.call-update) | async-done | bytes 3145744 | tf_op jit(solution)/shard_map/all_gather | solution.py:79
  150.1 133.1 %all-gather.7.cloned.1.call-done = bf16[1,4096,384]{1,2,0:T(8,128)(2,1)} async-done(((bf16[1,128,384]{1,2,0:T(8,128)(2,1)}), bf16[1,4096,384]{1,2,0:T(8,128)(2,1)}) %all-gather.7.cloned.1.call-update) | async-done | bytes 3145744 | tf_op jit(solution)/shard_map/all_gather | solution.py:80
  283.2 10.9 %conditional.2 = (f32[128,384]{0,1:T(8,128)S(1)}, bf16[128,384]{1,0:T(8,128)(2,1)S(1)}) conditional(s32[]{:T(128)} %convert_element_type.105, (f32[128,384]{0,1:T(8,128)S(1)}, bf16[4096,384]{0,1:T(8,128)(2,1)}, bf16[4096,384]{0,1:T(8,128)(2,1)}) %tuple.81, () %tuple.30), branch_computations={%region_1.8_spmd, %region_8.9_spmd} | conditional | flops 824670720 | bytes 58014736 | solution.py:96
  283.2 3.2 fusion.71
  286.5 0.8 fusion.76
  287.3 0.7 fusion
  288.1 0.9 fusion.39
  289.0 0.8 fusion.75
  289.8 0.7 fusion.2
  290.6 0.9 fusion.36
  291.5 0.8 fusion.74
  292.3 0.7 fusion.4
  293.0 0.9 fusion.33
  294.0 0.1 copy.15
  294.2 0.0 copy-start.6
  294.2 0.1 multiply_convert_fusion
  294.3 1.3 collective-permute-start
  295.6 2.2 collective-permute-done
  297.8 0.0 copy-done.6
  297.8 0.9 conditional.3
  297.8 0.7 broadcast.53.clone
  298.6 1.3 collective-permute-start.1
  299.9 1.6 select_bitcast_fusion
  301.5 39.4 %collective-permute-done.1 = bf16[128,384]{0,1:T(8,128)(2,1)S(1)} collective-permute-done((bf16[128,384]{0,1:T(8,128)(2,1)S(1)}, bf16[128,384]{0,1:T(8,128)(2,1)S(1)}, u32[]{:S(2)}, u32[]{:S(2)}) %collective-permute-start.1) | collective-permute-done | bytes 98336 | tf_op jit(solution)/shard_map/ppermute | solution.py:12
  340.9 0.1 multiply_reduce_fusion.3
  341.0 0.2 dynamic_update_slice.3
  341.3 7.2 %psum.14 = f32[768]{0:T(1024)S(1)} all-reduce(f32[768]{0:T(1024)S(1)} %dynamic_update_slice.3), channel_id=1, replica_groups=mesh['segment'=4,'seq'=32,'dp'=4] {'segment'}, use_global_device_ids=true, to_apply=%region_21.22 | all-reduce | flops 768 | bytes 6144 | tf_op jit(solution)/shard_map/psum | solution.py:120
  348.5 308.4 %psum.15 = f32[768]{0:T(1024)} all-reduce(f32[768]{0:T(1024)S(1)} %psum.14), channel_id=1, replica_groups=mesh['segment'=4,'seq'=32,'dp'=4] {'seq','dp'}, use_global_device_ids=true, to_apply=%region_22.23 | all-reduce | flops 768 | bytes 6144 | tf_op jit(solution)/shard_map/psum | solution.py:120
  (11 shorter events, 0.1 us)
Async XLA Ops:
  7.2 3.4 copy-start
  7.2 143.0 %all-gather.5.cloned.1.call-start = ((), (), s32[]{:S(2)}) async-start(), calls=%async_computation | async-start | bytes 3244032 | tf_op jit(solution)/shard_map/all_gather | solution.py:79
  8.9 274.4 %all-gather.7.cloned.1.call-start = ((), (), s32[]{:S(2)}) async-start(), calls=%async_computation.1 | async-start | bytes 3244032 | tf_op jit(solution)/shard_map/all_gather | solution.py:80
  294.2 3.6 copy-start.6
  294.3 3.5 collective-permute-start
  298.6 42.3 %collective-permute-start.1 = (bf16[128,384]{0,1:T(8,128)(2,1)S(1)}, bf16[128,384]{0,1:T(8,128)(2,1)S(1)}, u32[]{:S(2)}, u32[]{:S(2)}) collective-permute-start(bf16[128,384]{0,1:T(8,128)(2,1)S(1)} %get-tuple-element.53), channel_id=1, source_target_pairs={{256,0},{384,128},{257,1},{385,129},{258,2},{386,130},{259,3},{387... | collective-permute-start | bytes 294920 | tf_op jit(solution)/shard_map/ppermute | solution.py:12
Sparse Core Ops, SparseCore 0:
  10.6 139.4 all-gather.4
  152.1 131.0 all-gather.6
